TPU v7x, 32 devices: a whole 2x2x4 slice. The times are simulated.
32 devices in a mesh: field: 8 (over y, x, core), point: 4 (over z).
Axes of the slice: x: 2, y: 2, z: 4, core: 2. Of those that a mesh axis runs over, the one named last changes fastest.
Arguments:
- residual_in: bfloat16 [8, 1024, 2048], P('field', 'point'), may hold values from -6 to 6
- coefs_in: bfloat16 [8, 1024, 4, 256], P('field', 'point'), may hold values from 0 to 1
- dictionary: bfloat16 [2048, 2048], P('field'), may hold values from -0.125 to 0.125
- owner_order: int32 [8], replicated, may hold values from 0 to 7, each once
- pixel_of: int32 [8, 1024], P('field', 'point'), may hold values from 0 to 1023, each once within a row
Outputs:
- maps: float32 [8, 4, 256, 8, 128], P('field', None, 'point')
Inputs may be any that keep to these rules, and one draw needn't show every extreme that they name: `owner_order`: A permutation of the dictionary blocks. `pixel_of`: each field's row is a permutation of its scan points over the 8 x 128 pixels.
All inputs are finite; a program needn't handle non-finite values.
Results may differ from a plain program's by a relative error of at most 0.00045.
Values may be sent and summed in bfloat16 or wider, within the bound.
No kernel may reach another device: no remote copies, remote signals or barrier semaphores. Data moves between devices by JAX's collectives and lax.ppermute only.
A program may use at most 64 MiB of HBM per device.

v0:
```python
import jax
import jax.numpy as jnp
from jax import lax
from jax.sharding import PartitionSpec as P

TURNS = 4
SWEEPS = 4
MAP_W = 128
time_step = 0.2
edge_scale = 0.5


def from_root(value, axis, source):
    kept = jnp.where(lax.axis_index(axis) == source, value, 0).astype(value.dtype)
    return lax.psum(kept, axis)


def block_steps(templates):
    gram = lax.dot_general(
        templates, templates, (((1,), (1,)), ((), ())), preferred_element_type=jnp.float32
    )
    return 1.0 / jnp.sum(jnp.abs(gram), axis=1)


def diffuse(grids):
    for repeat in range(SWEEPS):
        padded = jnp.pad(grids, ((0, 0), (1, 1), (1, 1)), mode="edge")
        summed = jnp.zeros_like(grids)
        for neighbour in (
            padded[:, :-2, 1:-1],
            padded[:, 2:, 1:-1],
            padded[:, 1:-1, :-2],
            padded[:, 1:-1, 2:],
        ):
            differ = neighbour - grids
            scaled = differ / edge_scale
            summed = summed + differ / (1.0 + scaled * scaled)
        grids = grids + time_step * summed
    return grids


def build_maps(moved, pixel_ids):
    points = moved.shape[0]
    count = moved.shape[1]
    local_kb = moved.shape[2]
    values = moved.reshape(points, count * local_kb).T
    flat = jnp.zeros((count * local_kb, points), jnp.float32).at[:, pixel_ids].set(values)
    grids = diffuse(flat.reshape(count * local_kb, points // MAP_W, MAP_W))
    return grids.reshape(count, local_kb, points // MAP_W, MAP_W)


def per_device(residual_in, coefs_in, dictionary, owner_order, pixel_of):
    residual = residual_in[0]
    coefs = coefs_in[0].astype(jnp.float32)
    pixel_ids = lax.all_gather(pixel_of[0], "point", axis=0, tiled=True)
    own_steps = block_steps(dictionary)
    updated = []
    for turn_index in range(TURNS):
        owner = owner_order[turn_index]
        templates = from_root(dictionary, "field", owner)
        step_size = from_root(own_steps, "field", owner)
        correlation = lax.dot_general(
            residual, templates, (((1,), (1,)), ((), ())), preferred_element_type=jnp.float32
        )
        before = coefs[:, turn_index, :]
        after = jnp.maximum(before + step_size[None, :] * correlation, 0.0)
        updated.append(after)
        if turn_index + 1 < TURNS:
            change = (after - before).astype(jnp.bfloat16)
            residual = (
                residual.astype(jnp.float32)
                - jnp.dot(change, templates, preferred_element_type=jnp.float32)
            ).astype(jnp.bfloat16)
    stacked = jnp.stack(updated, axis=1)
    maps = build_maps(
        lax.all_to_all(stacked, "point", split_axis=2, concat_axis=0, tiled=True), pixel_ids
    )
    return maps[None]


def solution(mesh):
    placed = (
        P("field", "point", None),
        P("field", "point", None, None),
        P("field", None),
        P(),
        P("field", "point"),
    )
    return jax.shard_map(
        per_device,
        mesh=mesh,
        in_specs=placed,
        out_specs=P("field", None, "point", None, None),
        check_vma=False,
    )
```

profile of v0, /device:TPU:0, one launch (start us, length us, event | category | flops | bytes accessed | tf_op | source)
XLA Modules:
  0.0 157.1 jit_solution(16890992155468359398)
XLA Ops:
  6.5 0.0 all-reduce.4.cloned.1.call-start
  6.5 1.4 fusion.65
  10.4 3.3 %broadcast_select_fusion.3 = (bf16[256,2048]{1,0:T(8,128)(2,1)}, bf16[256,2048]{1,0:T(8,128)(2,1)}, bf16[256,2048]{1,0:T(8,128)(2,1)}, bf16[256,2048]{1,0:T(8,128)(2,1)}) fusion(bf16[256,2048]{1,0:T(8,128)(2,1)} %param.7, pred[]{:T(512)S(6)} %eq.16, pred[]{:T(512)S(6)} %eq.17, pred[]{:T(512)S(6)} %eq.19, pred[]{:T(512)S(6)} %eq.18), kind=kLoop, calls=%fused_computation.117 | loop fusion | flops 2097152 | bytes 5242884 | tf_op jit(solution)/shard_map/jit(_where)/select_n | solution.py:14
  13.8 0.0 copy-start.5
  13.8 0.0 all-reduce.4.cloned.1.call-update
  13.8 1.0 copy-done.5
  14.8 0.0 copy-start.3
  14.8 0.3 copy.19
  15.1 0.9 copy-done.3
  16.0 0.5 fusion.15
  16.5 0.0 copy-start
  16.6 16.0 %all-reduce = (f32[256]{0:T(256)S(1)}, f32[256]{0:T(256)S(1)}, f32[256]{0:T(256)S(1)}, f32[256]{0:T(256)S(1)}) all-reduce(f32[256]{0:T(256)S(1)} %get-tuple-element.29, f32[256]{0:T(256)S(1)} %get-tuple-element.28, f32[256]{0:T(256)S(1)} %get-tuple-element.27, ...), channel_id=1, replica_groups=mesh['field'=8,'point'=4] {'field'}, use_global_device_ids=true, to_apply=%region_1.2 | all-reduce | flops 1024 | bytes 8192 | tf_op jit(solution)/shard_map/psum | solution.py:15
  32.5 0.1 bitcast_convert_fusion
  32.6 65.1 %all-reduce.4.cloned.1.call-done = (bf16[256,2048]{1,0:T(8,128)(2,1)}, bf16[256,2048]{1,0:T(8,128)(2,1)}, bf16[256,2048]{1,0:T(8,128)(2,1)}, bf16[256,2048]{1,0:T(8,128)(2,1)}) async-done(((bf16[256,2048]{1,0:T(8,128)(2,1)}, bf16[256,2048]{1,0:T(8,128)(2,1)}, bf16[256,2048]{1,0:T(8,128)(2,1)}, bf16[256,2048]{1,0:T(8,128)(2,1)}), (bf16[256,2048]{1,0:T(8,128)(2,1)}, bf16[256,2048]{1,0:T(8,128)(2,1)}, ...) | async-done | bytes 4194320 | tf_op jit(solution)/shard_map/psum | solution.py:15
  97.7 0.0 copy-done
  97.7 0.0 copy-start.2
  97.7 1.8 %fusion.14 = f32[256,256]{0,1:T(8,128)S(1)} fusion(bf16[256,2048]{1,0:T(8,128)(2,1)} %get-tuple-element.12, bf16[1,256,2048]{2,1,0:T(8,128)(2,1)S(1)} %copy-done, f32[256,4,256]{0,2,1:T(8,128)S(1)} %bitcast_convert_fusion, f32[256]{0:T(256)S(1)} %get-tuple-element.5), kind=kOutput, calls=%fused_computation.37 | convolution fusion | flops 268632064 | bytes 2622464 | tf_op jit(solution)/shard_map/dot_general | solution.py:62
  99.5 0.0 copy-done.2
  99.5 0.0 copy-start.1
  99.6 0.5 fusion
  100.0 0.7 copy-done.1
  100.8 0.5 fusion.11
  101.2 0.0 copy-start.4
  101.3 0.5 fusion.1
  101.7 0.7 copy-done.4
  102.5 0.5 fusion.9
  103.0 2.5 %fusion.7 = f32[256,1,256]{0,2,1:T(8,128)S(1)} fusion(bf16[256,2048]{1,0:T(8,128)(2,1)} %get-tuple-element.9, bf16[256,2048]{1,0:T(8,128)(2,1)} %get-tuple-element.10, bf16[256,2048]{1,0:T(8,128)(2,1)S(1)} %fusion.1, f32[256,4,256]{0,2,1:T(8,128)S(1)} %bitcast_convert_fusion, f32[256,256]{0,1:T(8,128)S(1)} %fusion.9, f32[256]{0:T(256)S(1)} %get-tuple-element.8), kind=kOutput, calls=%fused_computation.27 | convolution fusion | flops 538771456 | bytes 4195328 | tf_op jit(solution)/shard_map/dot_general | solution.py:62
  105.4 0.1 pad_maximum_fusion.24
  105.5 1.6 %copy.23 = f32[256,4,256]{0,1,2:T(4,128)} copy(f32[256,4,256]{0,2,1:T(8,128)S(1)} %pad_maximum_fusion.24) | data formatting | bytes 2097152 | tf_op jit(solution)/shard_map/stack | solution.py:74
  107.2 0.0 copy-start.6
  107.2 4.7 %all-to-all-start = ((f32[256,4,256]{0,1,2:T(4,128)}), f32[256,4,256]{0,1,2:T(4,128)S(1)}, u32[]{:S(2)}, u32[]{:S(2)}) async-start(f32[256,4,256]{0,1,2:T(4,128)} %copy.23), calls=%async_computation | async-start | bytes 2097152 | tf_op jit(solution)/shard_map/all_to_all | solution.py:76
  111.9 0.0 copy-done.6
  111.9 22.7 %all-gather = s32[1,1024]{1,0:T(1,128)S(1)} all-gather(s32[1,256]{1,0:T(1,128)S(1)} %copy-done.6), channel_id=2, replica_groups=mesh['field'=8,'point'=4] {'point'}, dimensions={1}, use_global_device_ids=true | all-gather | bytes 5120 | tf_op jit(solution)/shard_map/all_gather | solution.py:55
  134.6 2.8 %all-to-all-done = f32[256,4,256]{0,1,2:T(4,128)S(1)} async-done(((f32[256,4,256]{0,1,2:T(4,128)}), f32[256,4,256]{0,1,2:T(4,128)S(1)}, u32[]{:S(2)}, u32[]{:S(2)}) %all-to-all-start) | async-done | bytes 1048608 | tf_op jit(solution)/shard_map/all_to_all | solution.py:76
  137.5 0.7 copy.24
  138.1 0.2 copy.30
  138.3 0.3 copy.25
  138.7 5.0 %scatter_custom_fusion = f32[256,1024]{0,1:T(8,128)S(1)} fusion(s32[1024]{0:T(1024)S(1)} %compare_select_fusion, f32[1024,256]{1,0:T(8,128)S(1)} %copy.25, f32[]{:T(128)} %constant.32.clone.1), kind=kCustom, calls=%fused_computation.119 | custom fusion | bytes 1048580 | tf_op jit(solution)/shard_map/scatter | solution.py:47
  143.8 1.3 multiply_add_fusion.3
  145.1 1.3 multiply_add_fusion.2
  146.4 1.3 multiply_add_fusion.1
  147.7 1.3 multiply_add_fusion
  149.0 1.3 copy.26
  (7 shorter events, 0.1 us)
Async XLA Ops:
  6.5 91.2 %all-reduce.4.cloned.1.call-start = ((), (), s32[]{:S(2)}) async-start(), calls=%async_computation.1 | async-start | bytes 8388608 | tf_op jit(solution)/shard_map/psum | solution.py:15
  13.8 1.0 copy-start.5
  14.8 1.2 copy-start.3
  16.5 81.2 %copy-start = (bf16[1,256,2048]{2,1,0:T(8,128)(2,1)S(1)}, bf16[1,256,2048]{2,1,0:T(8,128)(2,1)}, u32[]{:S(2)}) copy-start(bf16[1,256,2048]{2,1,0:T(8,128)(2,1)} %param.5) | copy-start | bytes 3145732
  97.7 1.8 %copy-start.2 = (bf16[256,2048]{1,0:T(8,128)(2,1)S(1)}, bf16[256,2048]{1,0:T(8,128)(2,1)}, u32[]{:S(2)}) copy-start(bf16[256,2048]{1,0:T(8,128)(2,1)} %get-tuple-element.12) | copy-start | bytes 3145732
  99.5 1.2 copy-start.1
  101.2 1.2 copy-start.4
  107.2 4.7 %copy-start.6 = (s32[1,256]{1,0:T(1,128)S(1)}, s32[1,256]{1,0:T(1,128)}, u32[]{:S(2)}) copy-start(s32[1,256]{1,0:T(1,128)} %param.9) | copy-start | bytes 3076
  107.2 30.3 %all-to-all-start = ((f32[256,4,256]{0,1,2:T(4,128)}), f32[256,4,256]{0,1,2:T(4,128)S(1)}, u32[]{:S(2)}, u32[]{:S(2)}) async-start(f32[256,4,256]{0,1,2:T(4,128)} %copy.23), calls=%async_computation | async-start | bytes 2097152 | tf_op jit(solution)/shard_map/all_to_all | solution.py:76
Sparse Core Ops, SparseCore 0:
  13.9 83.7 all-reduce.3
where the time goes:
time: 158 us; the launch traced here: 157 us
  waiting for transfers between devices  67.9 us (43%)
  blocking collectives  38.7 us (24%)
  between operations  16.1 us (10%)
  local copies, waits for them, and re-layouts  14.5 us (9%)
  other arithmetic  8.6 us (5%)
  matrix products  6.61 us (4%)
  starting transfers between devices  4.74 us (3%)
    psum x1, waiting for transfers between devices, from_root(): return lax.psum(kept, axis)  65.1 us
    all_gather x1, blocking collectives, per_device(): pixel_ids = lax.all_gather(pixel_of[0], 'point', axis=0, tiled=True)  22.7 us
    psum x1, blocking collectives, from_root(): return lax.psum(kept, axis)  16 us
    dot_general x4, matrix products, per_device(): lax.dot_general(residual, templates, (((1,), (1,)), ((), ())), preferred_...  5.2 us
    add x4, other arithmetic, diffuse(): grids = grids + time_step * summed  5.1 us
    scatter x1, local copies, waits for them, and re-layouts, build_maps(): jnp.zeros((count * local_kb, points), jnp.float32).at[:, pixel_ids]  5.05 us
    all_to_all x1, starting transfers between devices, per_device(): lax.all_to_all(stacked, 'point', split_axis=2, concat_axis=0, tiled=True)  4.74 us
    unnamed x16, local copies, waits for them, and re-layouts  3.94 us
  transfers between devices with their start and end apart: 2, of which 2 were waited for; matrix products, arithmetic and copies ran while one was open for 1% of the time, Pallas kernels for 0%

commit v1 on v0

--- a/solution.py
+++ b/solution.py
@@ -52,7 +52,14 @@
 def per_device(residual_in, coefs_in, dictionary, owner_order, pixel_of):
     residual = residual_in[0]
     coefs = coefs_in[0].astype(jnp.float32)
-    pixel_ids = lax.all_gather(pixel_of[0], "point", axis=0, tiled=True)
+    ring = [pixel_of[0]]
+    for hop in range(3):
+        ring.append(lax.ppermute(ring[-1], "point", [(dev, (dev + 1) % 4) for dev in range(4)]))
+    pixel_ids = jnp.roll(
+        jnp.concatenate(ring[::-1], axis=0),
+        (lax.axis_index("point") + 1) * ring[0].shape[0],
+        axis=0,
+    )
     own_steps = block_steps(dictionary)
     updated = []
     for turn_index in range(TURNS):

time: 158 us -> 164 us (1.038)
  blocking collectives: 38.7 us -> 16 us
  waiting for transfers between devices: 67.9 us -> 89.8 us
  starting transfers between devices: 4.74 us -> 11.7 us
    ppermute x0 -> x3, waiting for transfers between devices: none -> 24.7 us  [per_device(): lax.ppermute(ring[-1], 'point', [(dev, (dev + 1) % 4) for dev in range(4)])]
    all_gather x1 -> x0, blocking collectives: 22.7 us -> none  [per_device(): pixel_ids = lax.all_gather(pixel_of[0], 'point', axis=0, tiled=True)]
    ppermute x0 -> x3, starting transfers between devices: none -> 6.97 us  [per_device(): lax.ppermute(ring[-1], 'point', [(dev, (dev + 1) % 4) for dev in range(4)])]
    all_to_all x1, waiting for transfers between devices: 2.82 us -> 0.01 us  [per_device(): lax.all_to_all(stacked, 'point', split_axis=2, concat_axis=0, tiled=True)]
    unnamed x16 -> x23, local copies, waits for them, and re-layouts: 3.94 us -> 3.99 us
  transfers between devices with their start and end apart: 2 -> 5, of which waited for: 2 -> 4; matrix products, arithmetic and copies ran while one was open for 1% -> 1% of each run, Pallas kernels for 0% -> 0%
where the time goes in v1:
time: 164 us
  waiting for transfers between devices  89.8 us (55%)
  between operations  16.1 us (10%)
  blocking collectives  16 us (10%)
  local copies, waits for them, and re-layouts  14.7 us (9%)
  starting transfers between devices  11.7 us (7%)
  other arithmetic  8.69 us (5%)
  matrix products  6.61 us (4%)
    psum x1, waiting for transfers between devices, from_root(): return lax.psum(kept, axis)  65.1 us
    ppermute x3, waiting for transfers between devices, per_device(): lax.ppermute(ring[-1], 'point', [(dev, (dev + 1) % 4) for dev in range(4)])  24.7 us
    psum x1, blocking collectives, from_root(): return lax.psum(kept, axis)  16 us
    ppermute x3, starting transfers between devices, per_device(): lax.ppermute(ring[-1], 'point', [(dev, (dev + 1) % 4) for dev in range(4)])  6.97 us
    scatter x1, local copies, waits for them, and re-layouts, build_maps(): jnp.zeros((count * local_kb, points), jnp.float32).at[:, pixel_ids]  5.23 us
    dot_general x4, matrix products, per_device(): lax.dot_general(residual, templates, (((1,), (1,)), ((), ())), preferred_...  5.2 us
    add x4, other arithmetic, diffuse(): grids = grids + time_step * summed  5.09 us
    all_to_all x1, starting transfers between devices, per_device(): lax.all_to_all(stacked, 'point', split_axis=2, concat_axis=0, tiled=True)  4.74 us
  transfers between devices with their start and end apart: 5, of which 4 were waited for; matrix products, arithmetic and copies ran while one was open for 1% of the time, Pallas kernels for 0%

profile of v1, /device:TPU:0, one launch (start us, length us, event | category | flops | bytes accessed | tf_op | source)
XLA Modules:
  0.0 163.6 jit_solution(7518645076740975425)
XLA Ops:
  6.5 0.0 all-reduce.4.cloned.1.call-start
  6.5 1.4 fusion.65
  10.4 3.3 %broadcast_select_fusion.3 = (bf16[256,2048]{1,0:T(8,128)(2,1)}, bf16[256,2048]{1,0:T(8,128)(2,1)}, bf16[256,2048]{1,0:T(8,128)(2,1)}, bf16[256,2048]{1,0:T(8,128)(2,1)}) fusion(bf16[256,2048]{1,0:T(8,128)(2,1)} %param.7, pred[]{:T(512)S(6)} %eq.19, pred[]{:T(512)S(6)} %eq.20, pred[]{:T(512)S(6)} %eq.22, pred[]{:T(512)S(6)} %eq.21), kind=kLoop, calls=%fused_computation.117 | loop fusion | flops 2097152 | bytes 5242884 | tf_op jit(solution)/shard_map/jit(_where)/select_n | solution.py:14
  13.8 0.0 copy-start.5
  13.8 0.0 all-reduce.4.cloned.1.call-update
  13.8 1.0 copy-done.5
  14.8 0.0 copy-start.3
  14.8 0.3 copy.19
  15.2 0.9 copy-done.3
  16.0 0.5 fusion.15
  16.5 0.0 copy-start
  16.6 16.0 %all-reduce = (f32[256]{0:T(256)S(1)}, f32[256]{0:T(256)S(1)}, f32[256]{0:T(256)S(1)}, f32[256]{0:T(256)S(1)}) all-reduce(f32[256]{0:T(256)S(1)} %get-tuple-element.29, f32[256]{0:T(256)S(1)} %get-tuple-element.28, f32[256]{0:T(256)S(1)} %get-tuple-element.27, ...), channel_id=1, replica_groups=mesh['field'=8,'point'=4] {'field'}, use_global_device_ids=true, to_apply=%region_1.2 | all-reduce | flops 1024 | bytes 8192 | tf_op jit(solution)/shard_map/psum | solution.py:15
  32.6 0.1 bitcast_convert_fusion
  32.7 65.1 %all-reduce.4.cloned.1.call-done = (bf16[256,2048]{1,0:T(8,128)(2,1)}, bf16[256,2048]{1,0:T(8,128)(2,1)}, bf16[256,2048]{1,0:T(8,128)(2,1)}, bf16[256,2048]{1,0:T(8,128)(2,1)}) async-done(((bf16[256,2048]{1,0:T(8,128)(2,1)}, bf16[256,2048]{1,0:T(8,128)(2,1)}, bf16[256,2048]{1,0:T(8,128)(2,1)}, bf16[256,2048]{1,0:T(8,128)(2,1)}), (bf16[256,2048]{1,0:T(8,128)(2,1)}, bf16[256,2048]{1,0:T(8,128)(2,1)}, ...) | async-done | bytes 4194320 | tf_op jit(solution)/shard_map/psum | solution.py:15
  97.8 0.0 copy-done
  97.8 0.0 copy-start.2
  97.8 1.8 %fusion.14 = f32[256,256]{0,1:T(8,128)S(1)} fusion(bf16[256,2048]{1,0:T(8,128)(2,1)} %get-tuple-element.12, bf16[1,256,2048]{2,1,0:T(8,128)(2,1)S(1)} %copy-done, f32[256,4,256]{0,2,1:T(8,128)S(1)} %bitcast_convert_fusion, f32[256]{0:T(256)S(1)} %get-tuple-element.5), kind=kOutput, calls=%fused_computation.37 | convolution fusion | flops 268632064 | bytes 2622464 | tf_op jit(solution)/shard_map/dot_general | solution.py:69
  99.6 0.0 copy-done.2
  99.6 0.0 copy-start.1
  99.6 0.5 fusion
  100.0 0.7 copy-done.1
  100.8 0.5 fusion.11
  101.3 0.0 copy-start.4
  101.3 0.5 fusion.1
  101.8 0.7 copy-done.4
  102.5 0.5 fusion.9
  103.0 2.5 %fusion.7 = f32[256,1,256]{0,2,1:T(8,128)S(1)} fusion(bf16[256,2048]{1,0:T(8,128)(2,1)} %get-tuple-element.9, bf16[256,2048]{1,0:T(8,128)(2,1)} %get-tuple-element.10, bf16[256,2048]{1,0:T(8,128)(2,1)S(1)} %fusion.1, f32[256,4,256]{0,2,1:T(8,128)S(1)} %bitcast_convert_fusion, f32[256,256]{0,1:T(8,128)S(1)} %fusion.9, f32[256]{0:T(256)S(1)} %get-tuple-element.8), kind=kOutput, calls=%fused_computation.27 | convolution fusion | flops 538771456 | bytes 4195328 | tf_op jit(solution)/shard_map/dot_general | solution.py:69
  105.5 0.1 pad_maximum_fusion.24
  105.6 1.6 %copy.23 = f32[256,4,256]{0,1,2:T(4,128)} copy(f32[256,4,256]{0,2,1:T(8,128)S(1)} %pad_maximum_fusion.24) | data formatting | bytes 2097152 | tf_op jit(solution)/shard_map/stack | solution.py:81
  107.2 4.7 %all-to-all-start = ((f32[256,4,256]{0,1,2:T(4,128)}), f32[256,4,256]{0,1,2:T(4,128)S(1)}, u32[]{:S(2)}, u32[]{:S(2)}) async-start(f32[256,4,256]{0,1,2:T(4,128)} %copy.23), calls=%async_computation | async-start | bytes 2097152 | tf_op jit(solution)/shard_map/all_to_all | solution.py:83
  111.9 0.0 copy-done.6
  111.9 2.0 %collective-permute-start = (s32[256]{0:T(256)S(1)}, s32[256]{0:T(256)S(1)}, u32[]{:S(2)}, u32[]{:S(2)}) collective-permute-start(s32[256]{0:T(256)S(1)} %bitcast.77), channel_id=1, source_target_pairs={{0,1},{1,2},{2,3},{3,0},{4,5},{5,6},{6,7},{7,4},{8,9},{9,10},{10,1... | collective-permute-start | bytes 3080 | tf_op jit(solution)/shard_map/ppermute | solution.py:57
  114.0 18.9 %collective-permute-done = s32[256]{0:T(256)S(1)} collective-permute-done((s32[256]{0:T(256)S(1)}, s32[256]{0:T(256)S(1)}, u32[]{:S(2)}, u32[]{:S(2)}) %collective-permute-start) | collective-permute-done | bytes 1056 | tf_op jit(solution)/shard_map/ppermute | solution.py:57
  132.9 3.3 %collective-permute-start.1 = (s32[256]{0:T(256)S(1)}, s32[256]{0:T(256)S(1)}, u32[]{:S(2)}, u32[]{:S(2)}) collective-permute-start(s32[256]{0:T(256)S(1)} %collective-permute-done), channel_id=1, source_target_pairs={{0,1},{1,2},{2,3},{3,0},{4,5},{5,6},{6,7},{7,4},{8,9},{9,10},{10,1... | collective-permute-start | bytes 3080 | tf_op jit(solution)/shard_map/ppermute | solution.py:57
  136.2 2.1 %collective-permute-done.1 = s32[256]{0:T(256)S(1)} collective-permute-done((s32[256]{0:T(256)S(1)}, s32[256]{0:T(256)S(1)}, u32[]{:S(2)}, u32[]{:S(2)}) %collective-permute-start.1) | collective-permute-done | bytes 1056 | tf_op jit(solution)/shard_map/ppermute | solution.py:57
  138.2 1.6 collective-permute-start.2
  139.9 3.7 %collective-permute-done.2 = s32[256]{0:T(256)S(1)} collective-permute-done((s32[256]{0:T(256)S(1)}, s32[256]{0:T(256)S(1)}, u32[]{:S(2)}, u32[]{:S(2)}) %collective-permute-start.2) | collective-permute-done | bytes 1056 | tf_op jit(solution)/shard_map/ppermute | solution.py:57
  143.7 0.1 compare_select_fusion
  143.8 0.0 all-to-all-done
  143.8 0.7 copy.24
  144.5 0.2 copy.30
  144.7 0.3 copy.25
  145.0 5.2 %scatter_custom_fusion = f32[256,1024]{0,1:T(8,128)S(1)} fusion(s32[1024]{0:T(1024)S(1)} %compare_select_fusion, f32[1024,256]{1,0:T(8,128)S(1)} %copy.25, f32[]{:T(128)} %constant.54.clone.1), kind=kCustom, calls=%fused_computation.119 | custom fusion | bytes 1048580 | tf_op jit(solution)/shard_map/scatter | solution.py:47
  150.3 1.3 multiply_add_fusion.3
  151.6 1.3 multiply_add_fusion.2
  152.9 1.3 multiply_add_fusion.1
  154.2 1.3 multiply_add_fusion
  155.5 1.3 copy.26
  (16 shorter events, 0.1 us)
Async XLA Ops:
  6.5 91.2 %all-reduce.4.cloned.1.call-start = ((), (), s32[]{:S(2)}) async-start(), calls=%async_computation.1 | async-start | bytes 8388608 | tf_op jit(solution)/shard_map/psum | solution.py:15
  13.8 1.0 copy-start.5
  14.8 1.2 copy-start.3
  16.5 81.2 %copy-start = (bf16[1,256,2048]{2,1,0:T(8,128)(2,1)S(1)}, bf16[1,256,2048]{2,1,0:T(8,128)(2,1)}, u32[]{:S(2)}) copy-start(bf16[1,256,2048]{2,1,0:T(8,128)(2,1)} %param.5) | copy-start | bytes 3145732
  97.8 1.8 %copy-start.2 = (bf16[256,2048]{1,0:T(8,128)(2,1)S(1)}, bf16[256,2048]{1,0:T(8,128)(2,1)}, u32[]{:S(2)}) copy-start(bf16[256,2048]{1,0:T(8,128)(2,1)} %get-tuple-element.12) | copy-start | bytes 3145732
  99.6 1.2 copy-start.1
  101.3 1.2 copy-start.4
  107.2 4.7 %copy-start.6 = (s32[1,256]{1,0:T(1,128)S(1)}, s32[1,256]{1,0:T(1,128)}, u32[]{:S(2)}) copy-start(s32[1,256]{1,0:T(1,128)} %param.9) | copy-start | bytes 3076
  107.2 36.6 %all-to-all-start = ((f32[256,4,256]{0,1,2:T(4,128)}), f32[256,4,256]{0,1,2:T(4,128)S(1)}, u32[]{:S(2)}, u32[]{:S(2)}) async-start(f32[256,4,256]{0,1,2:T(4,128)} %copy.23), calls=%async_computation | async-start | bytes 2097152 | tf_op jit(solution)/shard_map/all_to_all | solution.py:83
  111.9 20.9 %collective-permute-start = (s32[256]{0:T(256)S(1)}, s32[256]{0:T(256)S(1)}, u32[]{:S(2)}, u32[]{:S(2)}) collective-permute-start(s32[256]{0:T(256)S(1)} %bitcast.77), channel_id=1, source_target_pairs={{0,1},{1,2},{2,3},{3,0},{4,5},{5,6},{6,7},{7,4},{8,9},{9,10},{10,1... | collective-permute-start | bytes 3080 | tf_op jit(solution)/shard_map/ppermute | solution.py:57
  132.9 5.4 %collective-permute-start.1 = (s32[256]{0:T(256)S(1)}, s32[256]{0:T(256)S(1)}, u32[]{:S(2)}, u32[]{:S(2)}) collective-permute-start(s32[256]{0:T(256)S(1)} %collective-permute-done), channel_id=1, source_target_pairs={{0,1},{1,2},{2,3},{3,0},{4,5},{5,6},{6,7},{7,4},{8,9},{9,10},{10,1... | collective-permute-start | bytes 3080 | tf_op jit(solution)/shard_map/ppermute | solution.py:57
  138.2 5.4 %collective-permute-start.2 = (s32[256]{0:T(256)S(1)}, s32[256]{0:T(256)S(1)}, u32[]{:S(2)}, u32[]{:S(2)}) collective-permute-start(s32[256]{0:T(256)S(1)} %collective-permute-done.1), channel_id=1, source_target_pairs={{0,1},{1,2},{2,3},{3,0},{4,5},{5,6},{6,7},{7,4},{8,9},{9,10},{10,1... | collective-permute-start | bytes 3080 | tf_op jit(solution)/shard_map/ppermute | solution.py:57
Sparse Core Ops, SparseCore 0:
  13.9 83.7 all-reduce.3
